TPU v7x, 128 devices: a whole 4x4x4 slice. The times are simulated.
128 devices in a mesh: comp: 4 (over x), blk: 32 (over y, z, core).
Axes of the slice: x: 4, y: 4, z: 4, core: 2. Of those that a mesh axis runs over, the one named last changes fastest.
Arguments:
- psi_start: float32 [4, 6, 256, 128, 128], P('comp', None, 'blk'), may hold values from -6 to 6
- adj_source: float32 [4, 6, 256, 128, 128], P('comp', None, 'blk'), may hold values from -6 to 6
- vol_inverse: float32 [4, 256, 128, 128], P('comp', 'blk'), may hold values from 0.5 to 2
- coupling: float32 [4, 6, 6, 6], P('comp'), may hold values from -0.6 to 0.65
- send_tile: int32 [128, 128, 8], P(('comp', 'blk')), may hold values from 0 to 1023
- send_count: int32 [128, 128], P(('comp', 'blk')), may hold values from 0 to 8, as said below
- send_weight: float32 [128, 128, 8], P(('comp', 'blk')), may hold values from 0.2 to 1
- recv_slot: int32 [128, 128, 8], P(('comp', 'blk')), may hold values from 0 to 63
- fringe_row: int32 [128, 64], P(('comp', 'blk')), may hold values from 0 to 1023, as said below
Outputs:
- psi_end: float32 [4, 6, 256, 128, 128], P('comp', None, 'blk')
Inputs may be any that keep to these rules, and one draw needn't show every extreme that they name: `send_count`: no tiles travel between devices of the same component; between devices of different components the count is 4 or more. In every draw one receiver gets 8 live entries from every device of the other components. `fringe_row`: the rows of one device's fringe slots are distinct.
All inputs are finite; a program needn't handle non-finite values.
Results may differ from a plain program's by a relative error of at most 0.0003.
Values sent between devices are 32-bit elements; how exact they have to be, the bound alone decides.
No kernel may reach another device: no remote copies, remote signals or barrier semaphores. Data moves between devices by JAX's collectives and lax.ppermute only.
A program may use at most 128 MiB of HBM per device.

v0:
```python
import jax
import jax.numpy as jnp
from jax import lax
from jax.sharding import PartitionSpec as P

PENALTY = 4.0
TIME_STEP = 0.08


def padded(cells, sides, width):
    for axis, dim in sides:
        count = lax.axis_size(axis)
        ends = count - 1
        head = lax.slice_in_dim(cells, 0, width, axis=dim)
        tail = lax.slice_in_dim(cells, cells.shape[dim] - width, cells.shape[dim], axis=dim)
        cells = jnp.concatenate(
            [
                lax.ppermute(tail, axis, [(i, (i + 1) % count) for i in range(ends)]),
                cells,
                lax.ppermute(head, axis, [((i + 1) % count, i) for i in range(ends)]),
            ],
            axis=dim,
        )
    return cells


def fringe_values(field, send_tile, send_count, send_weight, recv_slot, count_slots):
    nvar, depth, width, length = field.shape
    flat = field.reshape(nvar, depth * width, length)
    peers, capacity = send_tile.shape
    picked = jnp.take(flat, send_tile.reshape(-1), axis=1)
    live = lax.broadcasted_iota(jnp.int32, (peers, capacity), 1) < send_count.reshape(peers, 1)
    scale = jnp.where(live, send_weight, 0.0).reshape(-1)
    outgoing = (picked * scale[None, :, None]).reshape(nvar, peers, capacity, length)
    arrived = lax.all_to_all(outgoing, ("comp", "blk"), split_axis=1, concat_axis=1, tiled=True)
    arrived = arrived.reshape(nvar, peers * capacity, length)
    slot_ids = lax.broadcasted_iota(jnp.int32, (count_slots, 1), 0)
    onehot = (recv_slot.reshape(1, -1) == slot_ids).astype(jnp.float32)
    return jnp.einsum("sk,vkz->vsz", onehot, arrived, precision=lax.Precision.HIGHEST)


def apply_block(matrix, values):
    return jnp.einsum("vu,vxyz->uxyz", matrix, values, precision=lax.Precision.HIGHEST)


def residual_of(field, volume, source, matrices, interp, rows):
    nvar, depth, width, length = field.shape
    extended = padded(field, (("blk", 1),), 1)
    zero_y = jnp.zeros((nvar, depth, 1, length), jnp.float32)
    zero_z = jnp.zeros((nvar, depth, width, 1), jnp.float32)
    flux = apply_block(-jnp.sum(matrices, axis=0), field)
    flux = flux + apply_block(matrices[0], extended[:, 2:])
    flux = flux + apply_block(matrices[1], extended[:, :-2])
    flux = flux + apply_block(matrices[2], jnp.concatenate([field[:, :, 1:], zero_y], axis=2))
    flux = flux + apply_block(matrices[3], jnp.concatenate([zero_y, field[:, :, :-1]], axis=2))
    flux = flux + apply_block(matrices[4], jnp.concatenate([field[:, :, :, 1:], zero_z], axis=3))
    flux = flux + apply_block(matrices[5], jnp.concatenate([zero_z, field[:, :, :, :-1]], axis=3))
    rate = volume[None] * flux + source
    rate_flat = rate.reshape(nvar, depth * width, length)
    field_flat = field.reshape(nvar, depth * width, length)
    rate_flat = rate_flat.at[:, rows, :].add(PENALTY * (interp - field_flat[:, rows, :]))
    return rate_flat.reshape(nvar, depth, width, length)


def shards(
    psi_start,
    adj_source,
    vol_inverse,
    coupling,
    send_tile,
    send_count,
    send_weight,
    recv_slot,
    fringe_row,
):
    start = psi_start[0]
    source = adj_source[0]
    volume = vol_inverse[0]
    matrices = coupling[0]
    rows = fringe_row[0]

    def rate_of(field):
        interp = fringe_values(
            field, send_tile[0], send_count[0], send_weight[0], recv_slot[0], rows.shape[0]
        )
        return residual_of(field, volume, source, matrices, interp, rows)

    first = rate_of(start)
    middle = start + TIME_STEP * first
    second = rate_of(middle)
    result = start + 0.5 * TIME_STEP * (first + second)
    return result[None]


def solution(mesh):
    in_specs = (
        P("comp", None, "blk", None, None),
        P("comp", None, "blk", None, None),
        P("comp", "blk", None, None),
        P("comp", None, None, None),
        P(("comp", "blk"), None, None),
        P(("comp", "blk"), None),
        P(("comp", "blk"), None, None),
        P(("comp", "blk"), None, None),
        P(("comp", "blk"), None),
    )
    out_specs = P("comp", None, "blk", None, None)
    return jax.shard_map(shards, mesh=mesh, in_specs=in_specs, out_specs=out_specs, check_vma=False)
```

profile of v0, /device:TPU:1, one launch (start us, length us, event | category | flops | bytes accessed | tf_op | source)
XLA Modules:
  0.0 279.5 jit_solution(5447209523548036402)
XLA Ops:
  0.0 3.7 %copy.188 = f32[1,6,8,128,128]{4,1,3,2,0:T(8,128)S(1)} copy(f32[1,6,8,128,128]{4,3,2,1,0:T(8,128)} %param.11) | data formatting | bytes 6291456 | tf_op args[0]
  6.8 3.3 %collective-permute-start = (f32[6,1,128,128]{3,0,2,1:T(8,128)}, f32[6,1,128,128]{3,0,2,1:T(8,128)}, u32[]{:S(2)}, u32[]{:S(2)}) collective-permute-start(f32[6,1,128,128]{3,0,2,1:T(8,128)} %get-tuple-element.13), channel_id=1, source_target_pairs={{1,0},{2,1},{3,2},{4,3},{5,4},{6,5},{7,6},{8,7},{9,8},{10,9},{11,1... | collective-permute-start | bytes 1179656 | tf_op jit(solution)/shard_map/ppermute | solution.py:20
  10.1 3.5 %collective-permute-start.1 = (f32[6,1,128,128]{3,0,2,1:T(8,128)}, f32[6,1,128,128]{3,0,2,1:T(8,128)}, u32[]{:S(2)}, u32[]{:S(2)}) collective-permute-start(f32[6,1,128,128]{3,0,2,1:T(8,128)} %get-tuple-element.12), channel_id=1, source_target_pairs={{0,1},{1,2},{2,3},{3,4},{4,5},{5,6},{6,7},{7,8},{8,9},{9,10},{10,1... | collective-permute-start | bytes 1179656 | tf_op jit(solution)/shard_map/ppermute | solution.py:18
  14.3 10.4 %gather_fusion.2 = f32[1024,6,128]{2,1,0:T(8,128)} fusion(f32[6,1024,128]{2,0,1:T(8,128)} %bitcast.179, s32[1024]{0:T(1024)S(1)} %fusion.81), kind=kCustom, calls=%fused_computation.clone | custom fusion | bytes 6295552 | tf_op jit(solution)/shard_map/jit(_take)/gather | solution.py:31
  24.7 7.3 %bitcast_multiply_fusion.1 = f32[6,1024,128]{2,0,1:T(8,128)S(1)} fusion(f32[1024,6,128]{2,1,0:T(8,128)} %gather_fusion.2, f32[1024]{0:T(1024)S(1)} %broadcast_select_fusion, pred[1024]{0:T(1024)(128)(4,1)S(1)} %compare_and_fusion), kind=kLoop, calls=%fused_computation.32 | loop fusion | flops 1572864 | bytes 6296576 | tf_op jit(solution)/shard_map/mul | solution.py:34
  34.4 12.5 %all-to-all-start = ((f32[6,128,8,128]{3,2,0,1:T(8,128)}), f32[6,128,8,128]{3,2,0,1:T(8,128)}, u32[]{:S(2)}, u32[]{:S(2)}) async-start(f32[6,128,8,128]{3,2,0,1:T(8,128)} %copy.85), calls=%async_computation | async-start | bytes 6291456 | tf_op jit(solution)/shard_map/all_to_all | solution.py:35
  46.9 7.0 %fusion.94 = (f32[6,8,128,127]{3,0,2,1:T(8,128)}, f32[6,8,128,127]{3,0,2,1:T(8,128)S(1)}) fusion(f32[6,8,128,128]{3,0,2,1:T(8,128)} %bitcast.180), kind=kLoop, calls=%fused_computation.112 | loop fusion | bytes 12484608 | tf_op jit(solution)/shard_map/slice | solution.py:56
  53.9 5.2 %fusion.31 = f32[8,128,128,6]{2,3,1,0:T(8,128)} fusion(f32[6,8,128,128]{3,0,2,1:T(8,128)S(1)} %bitcast.184, f32[1,1,6,6]{3,0,2,1:T(1,128)S(1)} %get-tuple-element.20), kind=kOutput, calls=%fused_computation.53 | convolution fusion | flops 56180736 | bytes 7310336 | tf_op jit(solution)/shard_map/vu,vxyz->uxyz/dot_general | solution.py:43
  59.1 5.7 %fusion.23 = f32[8,128,128,6]{2,3,1,0:T(8,128)} fusion(f32[6,8,128,127]{3,0,2,1:T(8,128)S(1)} %get-tuple-element.15, f32[1,1,6,6]{3,0,2,1:T(1,128)S(1)} %get-tuple-element.23), kind=kOutput, calls=%fused_computation.45 | convolution fusion | flops 56623104 | bytes 6267024 | tf_op jit(solution)/shard_map/vu,vxyz->uxyz/dot_general | solution.py:43
  64.9 8.0 %fusion.33 = f32[8,128,128,6]{2,3,1,0:T(8,128)} fusion(f32[6,8,128,128]{3,0,2,1:T(8,128)} %bitcast.181, f32[1,1,6,6]{3,0,2,1:T(1,128)S(1)} %get-tuple-element.21), kind=kOutput, calls=%fused_computation.55 | convolution fusion | flops 56180736 | bytes 7307408 | tf_op jit(solution)/shard_map/vu,vxyz->uxyz/dot_general | solution.py:43
  72.9 7.4 %fusion.70 = f32[6,8,128,128]{3,0,2,1:T(8,128)} fusion(f32[1,6,8,128,128]{4,3,2,1,0:T(8,128)S(1)} %copy-done.4, f32[6,6]{1,0:T(8,128)S(1)} %reduce_sum.8), kind=kOutput, calls=%fused_computation.76 | convolution fusion | flops 56623140 | bytes 6291600 | tf_op jit(solution)/shard_map/vu,vxyz->uxyz/dot_general | solution.py:43
  80.3 5.3 %fusion.25 = f32[8,128,128,6]{2,3,1,0:T(8,128)} fusion(f32[6,8,128,127]{3,0,2,1:T(8,128)S(1)} %copy-done.6, f32[1,1,6,6]{3,0,2,1:T(1,128)S(1)} %get-tuple-element.19), kind=kOutput, calls=%fused_computation.47 | convolution fusion | flops 56623104 | bytes 6267024 | tf_op jit(solution)/shard_map/vu,vxyz->uxyz/dot_general | solution.py:43
  88.7 8.2 %fusion = f32[8,128,128,6]{2,3,1,0:T(8,128)} fusion(f32[6,1,128,128]{3,0,2,1:T(8,128)} %collective-permute-done, f32[6,8,128,128]{3,0,2,1:T(8,128)} %bitcast.183, f32[1,1,6,6]{3,0,2,1:T(1,128)S(1)} %get-tuple-element.22), kind=kOutput, calls=%fused_computation.6 | convolution fusion | flops 57507840 | bytes 6684816 | tf_op jit(solution)/shard_map/vu,vxyz->uxyz/dot_general | solution.py:43
  96.8 15.9 %bitcast_add_fusion.7 = f32[6,8,128,128]{3,0,2,1:T(8,128)} fusion(f32[1,6,8,128,128]{4,3,2,1,0:T(8,128)S(1)} %copy-done.5, f32[8,128,128,6]{2,3,1,0:T(8,128)} %fusion.23, f32[8,128,128,6]{2,3,1,0:T(8,128)} %fusion.25, f32[8,128,128,6]{2,3,1,0:T(8,128)} %fusion.31, f32[8,128,128,6]{2,3,1,0:T(8,128)} %fusion.33, f32[6,8,128,128]{3,0,2,1:T(8,128)} %fusion.70, ...), kind=kOutput, calls=%fused_computation.33 | convolution fusion | flops 63799296 | bytes 29229200 | tf_op jit(solution)/shard_map/vu,vxyz->uxyz/dot_general | solution.py:43
  112.8 3.2 %fusion.66 = f32[64,6,128]{2,0,1:T(8,128)S(1)} fusion(f32[6,128,8,128]{3,2,0,1:T(8,128)} %all-to-all-done, f32[64,6,128]{2,1,0:T(8,128)S(1)} %gather_fusion, s32[1024]{0:T(1024)S(1)} %eq.8), kind=kOutput, calls=%fused_computation.73 | convolution fusion | flops 604143616 | bytes 3543040 | tf_op jit(solution)/shard_map/sk,vkz->vsz/dot_general | solution.py:39
  116.1 6.8 %scatter_fusion = f32[6,1024,128]{2,0,1:T(8,128)} fusion(f32[6,1024,128]{2,0,1:T(8,128)} %bitcast.186, s32[64]{0:T(128)S(1)} %fusion.82, f32[64,6,128]{2,1,0:T(8,128)S(1)} %copy.89), kind=kCustom, calls=%fused_computation.4 | custom fusion | flops 49152 | bytes 590080 | tf_op jit(solution)/shard_map/scatter-add | solution.py:61
  129.1 5.4 %fusion.27 = f32[8,128,128,6]{2,3,1,0:T(8,128)} fusion(f32[6,8,128,128]{3,0,2,1:T(8,128)S(1)} %fusion.69, f32[1,1,6,6]{3,0,2,1:T(1,128)S(1)} %get-tuple-element.20), kind=kOutput, calls=%fused_computation.49 | convolution fusion | flops 56180736 | bytes 7310336 | tf_op jit(solution)/shard_map/vu,vxyz->uxyz/dot_general | solution.py:43
  134.5 5.1 %fusion.29 = f32[8,128,128,6]{2,3,1,0:T(8,128)} fusion(f32[6,8,128,128]{3,0,2,1:T(8,128)S(1)} %fusion.69, f32[1,1,6,6]{3,0,2,1:T(1,128)S(1)} %get-tuple-element.21), kind=kOutput, calls=%fused_computation.51 | convolution fusion | flops 56180736 | bytes 7310336 | tf_op jit(solution)/shard_map/vu,vxyz->uxyz/dot_general | solution.py:43
  139.6 5.8 %fusion.76 = f32[6,8,128,128]{3,0,2,1:T(8,128)} fusion(f32[6,8,128,128]{3,0,2,1:T(8,128)S(1)} %fusion.69, f32[6,6]{1,0:T(8,128)S(1)} %reduce_sum.8), kind=kOutput, calls=%fused_computation.90 | convolution fusion | flops 56623140 | bytes 6291600 | tf_op jit(solution)/shard_map/vu,vxyz->uxyz/dot_general | solution.py:43
  145.4 2.8 %collective-permute-start.2 = (f32[6,1,128,128]{3,0,2,1:T(8,128)S(1)}, f32[6,1,128,128]{3,0,2,1:T(8,128)S(1)}, u32[]{:S(2)}, u32[]{:S(2)}) collective-permute-start(f32[6,1,128,128]{3,0,2,1:T(8,128)S(1)} %get-tuple-element.9), channel_id=1, source_target_pairs={{1,0},{2,1},{3,2},{4,3},{5,4},{6,5},{7,6},{8,7},{9,8},{10,9},{11,1... | collective-permute-start | bytes 1179656 | tf_op jit(solution)/shard_map/ppermute | solution.py:20
  148.2 5.3 %fusion.21 = f32[8,128,128,6]{2,3,1,0:T(8,128)} fusion(f32[6,8,128,127]{3,0,2,1:T(8,128)S(1)} %get-tuple-element.10, f32[1,1,6,6]{3,0,2,1:T(1,128)S(1)} %get-tuple-element.19), kind=kOutput, calls=%fused_computation.43 | convolution fusion | flops 56623104 | bytes 6267024 | tf_op jit(solution)/shard_map/vu,vxyz->uxyz/dot_general | solution.py:43
  156.3 5.9 %fusion.19 = f32[8,128,128,6]{2,3,1,0:T(8,128)} fusion(f32[6,8,128,127]{3,0,2,1:T(8,128)S(1)} %get-tuple-element.11, f32[1,1,6,6]{3,0,2,1:T(1,128)S(1)} %get-tuple-element.23), kind=kOutput, calls=%fused_computation.41 | convolution fusion | flops 56623104 | bytes 6267024 | tf_op jit(solution)/shard_map/vu,vxyz->uxyz/dot_general | solution.py:43
  162.3 5.8 %fusion.8 = f32[8,128,128,6]{2,3,1,0:T(8,128)} fusion(f32[6,1,128,128]{3,0,2,1:T(8,128)S(1)} %collective-permute-done.2, f32[6,8,128,128]{3,0,2,1:T(8,128)S(1)} %fusion.69, f32[1,1,6,6]{3,0,2,1:T(1,128)S(1)} %get-tuple-element.22), kind=kOutput, calls=%fused_computation.14 | convolution fusion | flops 57507840 | bytes 6684816 | tf_op jit(solution)/shard_map/vu,vxyz->uxyz/dot_general | solution.py:43
  168.1 14.1 %fusion.17 = f32[6,8,128,128]{3,0,2,1:T(8,128)} fusion(f32[8,128,128,6]{2,3,1,0:T(8,128)} %fusion.19, f32[8,128,128,6]{2,3,1,0:T(8,128)} %fusion.21, f32[8,128,128,6]{2,3,1,0:T(8,128)} %fusion.27, f32[8,128,128,6]{2,3,1,0:T(8,128)} %fusion.29, f32[6,8,128,128]{3,0,2,1:T(8,128)} %fusion.76, f32[8,128,128,6]{2,3,1,0:T(8,128)} %fusion.8, ...), kind=kOutput, calls=%fused_computation.26 | convolution fusion | flops 63799296 | bytes 29229200 | tf_op jit(solution)/shard_map/vu,vxyz->uxyz/dot_general | solution.py:43
  182.2 7.9 %bitcast_add_fusion.14 = (f32[6,1024,128]{2,0,1:T(8,128)}, f32[6,1024,128]{2,0,1:T(8,128)}) fusion(f32[1,6,8,128,128]{4,1,3,2,0:T(8,128)S(1)} %copy-done.3, f32[6,1024,128]{2,0,1:T(8,128)} %scatter_fusion, f32[6,8,128,128]{3,0,2,1:T(8,128)} %fusion.17), kind=kLoop, calls=%fused_computation.104 | loop fusion | flops 2359296 | bytes 15728640 | tf_op jit(solution)/shard_map/add | solution.py:89
  190.1 10.4 %gather_fusion.3 = f32[1024,6,128]{2,1,0:T(8,128)} fusion(f32[6,1024,128]{2,0,1:T(8,128)} %get-tuple-element.6, s32[1024]{0:T(1024)S(1)} %fusion.81), kind=kCustom, calls=%fused_computation.1.clone | custom fusion | bytes 6295552 | tf_op jit(solution)/shard_map/jit(_take)/gather | solution.py:31
  200.5 7.3 %bitcast_multiply_fusion = f32[6,1024,128]{2,0,1:T(8,128)S(1)} fusion(f32[1024,6,128]{2,1,0:T(8,128)} %gather_fusion.3, f32[1024]{0:T(1024)S(1)} %broadcast_select_fusion, pred[1024]{0:T(1024)(128)(4,1)S(1)} %compare_and_fusion), kind=kLoop, calls=%fused_computation.22 | loop fusion | flops 1572864 | bytes 6296576 | tf_op jit(solution)/shard_map/mul | solution.py:34
  210.3 12.4 %all-to-all-start.1 = ((f32[6,128,8,128]{3,2,0,1:T(8,128)}), f32[6,128,8,128]{3,2,0,1:T(8,128)}, u32[]{:S(2)}, u32[]{:S(2)}) async-start(f32[6,128,8,128]{3,2,0,1:T(8,128)} %copy.97), calls=%async_computation.1 | async-start | bytes 6291456 | tf_op jit(solution)/shard_map/all_to_all | solution.py:35
  222.6 2.8 gather_fusion.1
  225.4 38.6 %all-to-all-done.1 = f32[6,128,8,128]{3,2,0,1:T(8,128)} async-done(((f32[6,128,8,128]{3,2,0,1:T(8,128)}), f32[6,128,8,128]{3,2,0,1:T(8,128)}, u32[]{:S(2)}, u32[]{:S(2)}) %all-to-all-start.1) | async-done | bytes 3145760 | tf_op jit(solution)/shard_map/all_to_all | solution.py:35
  264.0 3.2 %fusion.57 = f32[64,6,128]{2,0,1:T(8,128)S(1)} fusion(f32[6,128,8,128]{3,2,0,1:T(8,128)} %all-to-all-done.1, f32[64,6,128]{2,1,0:T(8,128)S(1)} %gather_fusion.1, s32[1024]{0:T(1024)S(1)} %eq.8), kind=kOutput, calls=%fused_computation.70 | convolution fusion | flops 604143616 | bytes 3543040 | tf_op jit(solution)/shard_map/sk,vkz->vsz/dot_general | solution.py:39
  267.3 6.8 %scatter_fusion.1 = f32[6,1024,128]{2,0,1:T(8,128)} fusion(f32[6,1024,128]{2,0,1:T(8,128)} %get-tuple-element.7, s32[64]{0:T(128)S(1)} %fusion.82, f32[64,6,128]{2,1,0:T(8,128)S(1)} %copy.100), kind=kCustom, calls=%fused_computation.5 | custom fusion | flops 49152 | bytes 590080 | tf_op jit(solution)/shard_map/scatter-add | solution.py:61
  (63 shorter events, 25.9 us)
Async XLA Ops:
  0.0 13.6 %copy-start.10 = (s32[1,128,8]{1,2,0:T(8,128)S(1)}, s32[1,128,8]{1,2,0:T(8,128)}, u32[]{:S(2)}) copy-start(s32[1,128,8]{1,2,0:T(8,128)} %param.15) | copy-start | bytes 12292
  0.0 13.9 %copy-start.11 = (f32[1,128,8]{1,2,0:T(8,128)S(1)}, f32[1,128,8]{1,2,0:T(8,128)}, u32[]{:S(2)}) copy-start(f32[1,128,8]{1,2,0:T(8,128)} %param.17) | copy-start | bytes 12292
  0.0 14.1 %copy-start.13 = (s32[1,128]{1,0:T(1,128)S(1)}, s32[1,128]{1,0:T(1,128)}, u32[]{:S(2)}) copy-start(s32[1,128]{1,0:T(1,128)} %param.16) | copy-start | bytes 1540
  3.7 1.9 copy-start
  6.8 81.8 %collective-permute-start = (f32[6,1,128,128]{3,0,2,1:T(8,128)}, f32[6,1,128,128]{3,0,2,1:T(8,128)}, u32[]{:S(2)}, u32[]{:S(2)}) collective-permute-start(f32[6,1,128,128]{3,0,2,1:T(8,128)} %get-tuple-element.13), channel_id=1, source_target_pairs={{1,0},{2,1},{3,2},{4,3},{5,4},{6,5},{7,6},{8,7},{9,8},{10,9},{11,1... | collective-permute-start | bytes 1179656 | tf_op jit(solution)/shard_map/ppermute | solution.py:20
  10.1 86.7 %collective-permute-start.1 = (f32[6,1,128,128]{3,0,2,1:T(8,128)}, f32[6,1,128,128]{3,0,2,1:T(8,128)}, u32[]{:S(2)}, u32[]{:S(2)}) collective-permute-start(f32[6,1,128,128]{3,0,2,1:T(8,128)} %get-tuple-element.12), channel_id=1, source_target_pairs={{0,1},{1,2},{2,3},{3,4},{4,5},{5,6},{6,7},{7,8},{8,9},{9,10},{10,1... | collective-permute-start | bytes 1179656 | tf_op jit(solution)/shard_map/ppermute | solution.py:18
  34.4 78.4 %all-to-all-start = ((f32[6,128,8,128]{3,2,0,1:T(8,128)}), f32[6,128,8,128]{3,2,0,1:T(8,128)}, u32[]{:S(2)}, u32[]{:S(2)}) async-start(f32[6,128,8,128]{3,2,0,1:T(8,128)} %copy.85), calls=%async_computation | async-start | bytes 6291456 | tf_op jit(solution)/shard_map/all_to_all | solution.py:35
  46.9 7.0 %copy-start.9 = (f32[1,6,6,6]{3,0,2,1:T(1,128)S(1)}, f32[1,6,6,6]{3,0,2,1:T(1,128)}, u32[]{:S(2)}) copy-start(f32[1,6,6,6]{3,0,2,1:T(1,128)} %param.14) | copy-start | bytes 2596
  46.9 7.0 %copy-start.1 = (f32[1,6,8,128,128]{4,1,3,2,0:T(8,128)S(1)}, f32[1,6,8,128,128]{4,1,3,2,0:T(8,128)}, u32[]{:S(2)}) copy-start(f32[1,6,8,128,128]{4,1,3,2,0:T(8,128)} %copy-done) | copy-start | bytes 9437188
  59.1 5.7 %copy-start.14 = (s32[1,64]{1,0:T(1,128)S(1)}, s32[1,64]{1,0:T(1,128)}, u32[]{:S(2)}) copy-start(s32[1,64]{1,0:T(1,128)} %param.19) | copy-start | bytes 772
  64.8 8.0 %copy-start.4 = (f32[1,6,8,128,128]{4,3,2,1,0:T(8,128)S(1)}, f32[1,6,8,128,128]{4,3,2,1,0:T(8,128)}, u32[]{:S(2)}) copy-start(f32[1,6,8,128,128]{4,3,2,1,0:T(8,128)} %param.11) | copy-start | bytes 9437188
  72.9 7.4 %copy-start.6 = (f32[6,8,128,127]{3,0,2,1:T(8,128)S(1)}, f32[6,8,128,127]{3,0,2,1:T(8,128)}, u32[]{:S(2)}) copy-start(f32[6,8,128,127]{3,0,2,1:T(8,128)} %get-tuple-element.14) | copy-start | bytes 9363460
  80.3 8.1 %copy-start.12 = (s32[1,128,8]{1,2,0:T(8,128)S(1)}, s32[1,128,8]{1,2,0:T(8,128)}, u32[]{:S(2)}) copy-start(s32[1,128,8]{1,2,0:T(8,128)} %param.18) | copy-start | bytes 12292
  88.6 8.2 %copy-start.2 = (f32[1,6,8,128,128]{4,1,3,2,0:T(8,128)S(1)}, f32[1,6,8,128,128]{4,1,3,2,0:T(8,128)}, u32[]{:S(2)}) copy-start(f32[1,6,8,128,128]{4,1,3,2,0:T(8,128)} %copy-done) | copy-start | bytes 9437188
  88.6 8.2 %copy-start.5 = (f32[1,6,8,128,128]{4,3,2,1,0:T(8,128)S(1)}, f32[1,6,8,128,128]{4,3,2,1,0:T(8,128)}, u32[]{:S(2)}) copy-start(f32[1,6,8,128,128]{4,3,2,1,0:T(8,128)} %param.12) | copy-start | bytes 9437188
  88.6 8.2 %copy-start.7 = (f32[1,8,128,128]{3,2,1,0:T(8,128)S(1)}, f32[1,8,128,128]{3,2,1,0:T(8,128)}, u32[]{:S(2)}) copy-start(f32[1,8,128,128]{3,2,1,0:T(8,128)} %param.13) | copy-start | bytes 1572868
  145.4 16.9 %collective-permute-start.2 = (f32[6,1,128,128]{3,0,2,1:T(8,128)S(1)}, f32[6,1,128,128]{3,0,2,1:T(8,128)S(1)}, u32[]{:S(2)}, u32[]{:S(2)}) collective-permute-start(f32[6,1,128,128]{3,0,2,1:T(8,128)S(1)} %get-tuple-element.9), channel_id=1, source_target_pairs={{1,0},{2,1},{3,2},{4,3},{5,4},{6,5},{7,6},{8,7},{9,8},{10,9},{11,1... | collective-permute-start | bytes 1179656 | tf_op jit(solution)/shard_map/ppermute | solution.py:20
  153.6 14.5 %collective-permute-start.3 = (f32[6,1,128,128]{3,0,2,1:T(8,128)S(1)}, f32[6,1,128,128]{3,0,2,1:T(8,128)S(1)}, u32[]{:S(2)}, u32[]{:S(2)}) collective-permute-start(f32[6,1,128,128]{3,0,2,1:T(8,128)S(1)} %get-tuple-element.8), channel_id=1, source_target_pairs={{0,1},{1,2},{2,3},{3,4},{4,5},{5,6},{6,7},{7,8},{8,9},{9,10},{10,1... | collective-permute-start | bytes 1179656 | tf_op jit(solution)/shard_map/ppermute | solution.py:18
  162.3 5.8 %copy-start.8 = (f32[1,8,128,128]{3,2,1,0:T(8,128)S(1)}, f32[1,8,128,128]{3,2,1,0:T(8,128)}, u32[]{:S(2)}) copy-start(f32[1,8,128,128]{3,2,1,0:T(8,128)} %param.13) | copy-start | bytes 1572868
  168.1 14.1 %copy-start.3 = (f32[1,6,8,128,128]{4,1,3,2,0:T(8,128)S(1)}, f32[1,6,8,128,128]{4,1,3,2,0:T(8,128)}, u32[]{:S(2)}) copy-start(f32[1,6,8,128,128]{4,1,3,2,0:T(8,128)} %copy-done) | copy-start | bytes 9437188
  210.3 53.7 %all-to-all-start.1 = ((f32[6,128,8,128]{3,2,0,1:T(8,128)}), f32[6,128,8,128]{3,2,0,1:T(8,128)}, u32[]{:S(2)}, u32[]{:S(2)}) async-start(f32[6,128,8,128]{3,2,0,1:T(8,128)} %copy.97), calls=%async_computation.1 | async-start | bytes 6291456 | tf_op jit(solution)/shard_map/all_to_all | solution.py:35
where the time goes:
time: 284 us; the launch traced here: 279 us
  matrix products  110 us (39%)
  local copies, waits for them, and re-layouts  47.3 us (17%)
  other arithmetic  46.2 us (16%)
  waiting for transfers between devices  38.6 us (14%)
  starting transfers between devices  37.3 us (13%)
    dot_general x14, matrix products, apply_block(): jnp.einsum('vu,vxyz->uxyz', matrix, values, precision=lax.Precision.HIGHEST)  103 us
    all_to_all x2, waiting for transfers between devices, fringe_values(): lax.all_to_all(outgoing, ('comp', 'blk'), split_axis=1, concat_axis=1, ti...  38.6 us
    all_to_all x2, starting transfers between devices, fringe_values(): lax.all_to_all(outgoing, ('comp', 'blk'), split_axis=1, concat_axis=1, ti...  24.9 us
    gather x2, local copies, waits for them, and re-layouts, fringe_values(): picked = jnp.take(flat, send_tile.reshape(-1), axis=1)  20.8 us
    mul x2, other arithmetic, fringe_values(): picked * scale[None, :, None]  14.6 us
    scatter-add x2, other arithmetic, residual_of(): rate_flat.at[:, rows, :].add(PENALTY * (interp - field_flat[:, rows, :]))  13.6 us
    add x2, other arithmetic, shards(): middle = start + TIME_STEP * first  10 us
    slice x2, local copies, waits for them, and re-layouts, residual_of(): field[:, :, :, 1:]  8.32 us
  transfers between devices with their start and end apart: 6, of which 1 were waited for; matrix products, arithmetic and copies ran while one was open for 38% of the time, Pallas kernels for 0%

commit v1 on v0

--- a/solution.py
+++ b/solution.py
@@ -32,7 +32,14 @@
     live = lax.broadcasted_iota(jnp.int32, (peers, capacity), 1) < send_count.reshape(peers, 1)
     scale = jnp.where(live, send_weight, 0.0).reshape(-1)
     outgoing = (picked * scale[None, :, None]).reshape(nvar, peers, capacity, length)
-    arrived = lax.all_to_all(outgoing, ("comp", "blk"), split_axis=1, concat_axis=1, tiled=True)
+
+    def _bring_matrix(raw, ax_name):
+        value_now = jnp.stack(jnp.split(raw, jax.lax.axis_size(ax_name), axis=1), axis=0)
+        z = jax.lax.all_to_all(value_now, ax_name, 0, 0)
+        x_new = jnp.concatenate(z, axis=1)
+        return x_new
+
+    arrived = _bring_matrix(outgoing, ("comp", "blk"))
     arrived = arrived.reshape(nvar, peers * capacity, length)
     slot_ids = lax.broadcasted_iota(jnp.int32, (count_slots, 1), 0)
     onehot = (recv_slot.reshape(1, -1) == slot_ids).astype(jnp.float32)

time: 284 us -> 442 us (1.56)
  local copies, waits for them, and re-layouts: 47.3 us -> 202 us
    unnamed x34 -> x284, local copies, waits for them, and re-layouts: 6.03 us -> 162 us
    reshape x2 -> x0, local copies, waits for them, and re-layouts: 4.84 us -> none  [fringe_values(): (picked * scale[None, :, None]).reshape(nvar, peers, capacity, length)]
  transfers between devices with their start and end apart: 6 -> 6, of which waited for: 1 -> 1; matrix products, arithmetic and copies ran while one was open for 38% -> 20% of each run, Pallas kernels for 0% -> 0%
where the time goes in v1:
time: 442 us; the launch traced here: 435 us
  local copies, waits for them, and re-layouts  202 us (46%)
  matrix products  110 us (25%)
  other arithmetic  46.4 us (10%)
  waiting for transfers between devices  38.8 us (9%)
  starting transfers between devices  37.4 us (8%)
    unnamed x284, local copies, waits for them, and re-layouts  162 us
    dot_general x14, matrix products, apply_block(): jnp.einsum('vu,vxyz->uxyz', matrix, values, precision=lax.Precision.HIGHEST)  104 us
    all_to_all x2, waiting for transfers between devices, _bring_matrix(): z = jax.lax.all_to_all(value_now, ax_name, 0, 0)  38.8 us
    all_to_all x2, starting transfers between devices, _bring_matrix(): z = jax.lax.all_to_all(value_now, ax_name, 0, 0)  26 us
    gather x2, local copies, waits for them, and re-layouts, fringe_values(): picked = jnp.take(flat, send_tile.reshape(-1), axis=1)  20.8 us
    mul x2, other arithmetic, fringe_values(): picked * scale[None, :, None]  14.9 us
    scatter-add x2, other arithmetic, residual_of(): rate_flat.at[:, rows, :].add(PENALTY * (interp - field_flat[:, rows, :]))  13.5 us
    add x2, other arithmetic, shards(): middle = start + TIME_STEP * first  10.1 us
  transfers between devices with their start and end apart: 6, of which 1 were waited for; matrix products, arithmetic and copies ran while one was open for 20% of the time, Pallas kernels for 0%

profile of v1, /device:TPU:1, one launch (start us, length us, event | category | flops | bytes accessed | tf_op | source)
XLA Modules:
  0.0 435.3 jit_solution(7182401021654842179)
XLA Ops:
  0.9 5.7 %copy.1974 = f32[1,6,8,128,128]{4,1,3,2,0:T(8,128)} copy(f32[1,6,8,128,128]{4,3,2,1,0:T(8,128)} %param.11) | data formatting | bytes 6291456 | tf_op args[0]
  7.0 10.4 %gather_fusion.2 = f32[1024,6,128]{2,1,0:T(8,128)} fusion(f32[6,1024,128]{2,0,1:T(8,128)} %bitcast.1210, s32[1024]{0:T(1024)S(1)} %fusion.81), kind=kCustom, calls=%fused_computation.clone | custom fusion | bytes 6295552 | tf_op jit(solution)/shard_map/jit(_take)/gather | solution.py:31
  17.4 7.3 %bitcast_multiply_fusion.1 = f32[6,1024,128]{2,0,1:T(8,128)S(1)} fusion(f32[1024,6,128]{2,1,0:T(8,128)} %gather_fusion.2, f32[1024]{0:T(1024)S(1)} %broadcast_select_fusion, pred[1024]{0:T(1024)(128)(4,1)S(1)} %compare_and_fusion), kind=kLoop, calls=%fused_computation.32 | loop fusion | flops 1572864 | bytes 6296576 | tf_op jit(solution)/shard_map/mul | solution.py:34
  103.6 11.9 %all-to-all-start = ((f32[128,6,1,8,128]{4,3,1,2,0:T(8,128)}), f32[128,6,1,8,128]{4,3,1,2,0:T(8,128)}, u32[]{:S(2)}, u32[]{:S(2)}) async-start(f32[128,6,1,8,128]{4,3,1,2,0:T(8,128)} %constant_dynamic-update-slice_fusion), calls=%async_computation | async-start | bytes 6291456 | tf_op jit(solution)/shard_map/all_to_all | solution.py:38
  117.8 3.0 collective-permute-start
  120.9 2.8 collective-permute-start.1
  123.7 6.9 %fusion.108 = (f32[6,8,128,127]{3,0,2,1:T(8,128)}, f32[6,8,128,127]{3,0,2,1:T(8,128)S(1)}) fusion(f32[6,8,128,128]{3,0,2,1:T(8,128)} %bitcast.1212), kind=kLoop, calls=%fused_computation.638 | loop fusion | bytes 12484608 | tf_op jit(solution)/shard_map/slice | solution.py:63
  130.6 5.5 %fusion.31 = f32[8,128,128,6]{2,3,1,0:T(8,128)} fusion(f32[6,8,128,128]{3,0,2,1:T(8,128)S(1)} %bitcast.1216, f32[1,1,6,6]{3,0,2,1:T(1,128)S(1)} %get-tuple-element.276), kind=kOutput, calls=%fused_computation.53 | convolution fusion | flops 56180736 | bytes 7310336 | tf_op jit(solution)/shard_map/vu,vxyz->uxyz/dot_general | solution.py:50
  136.0 5.7 %fusion.23 = f32[8,128,128,6]{2,3,1,0:T(8,128)} fusion(f32[6,8,128,127]{3,0,2,1:T(8,128)S(1)} %get-tuple-element.271, f32[1,1,6,6]{3,0,2,1:T(1,128)S(1)} %get-tuple-element.279), kind=kOutput, calls=%fused_computation.45 | convolution fusion | flops 56623104 | bytes 6267024 | tf_op jit(solution)/shard_map/vu,vxyz->uxyz/dot_general | solution.py:50
  141.8 8.0 %fusion.33 = f32[8,128,128,6]{2,3,1,0:T(8,128)} fusion(f32[6,8,128,128]{3,0,2,1:T(8,128)} %bitcast.1213, f32[1,1,6,6]{3,0,2,1:T(1,128)S(1)} %get-tuple-element.277), kind=kOutput, calls=%fused_computation.55 | convolution fusion | flops 56180736 | bytes 7307408 | tf_op jit(solution)/shard_map/vu,vxyz->uxyz/dot_general | solution.py:50
  149.8 7.2 %fusion.70 = f32[6,8,128,128]{3,0,2,1:T(8,128)} fusion(f32[1,6,8,128,128]{4,3,2,1,0:T(8,128)S(1)} %copy-done.3, f32[6,6]{1,0:T(8,128)S(1)} %reduce_sum.8), kind=kOutput, calls=%fused_computation.332 | convolution fusion | flops 56623140 | bytes 6291600 | tf_op jit(solution)/shard_map/vu,vxyz->uxyz/dot_general | solution.py:50
  157.1 5.8 %fusion.25 = f32[8,128,128,6]{2,3,1,0:T(8,128)} fusion(f32[6,8,128,127]{3,0,2,1:T(8,128)S(1)} %copy-done.5, f32[1,1,6,6]{3,0,2,1:T(1,128)S(1)} %get-tuple-element.275), kind=kOutput, calls=%fused_computation.47 | convolution fusion | flops 56623104 | bytes 6267024 | tf_op jit(solution)/shard_map/vu,vxyz->uxyz/dot_general | solution.py:50
  165.9 8.2 %fusion = f32[8,128,128,6]{2,3,1,0:T(8,128)} fusion(f32[6,1,128,128]{3,0,2,1:T(8,128)} %collective-permute-done, f32[6,8,128,128]{3,0,2,1:T(8,128)} %bitcast.1215, f32[1,1,6,6]{3,0,2,1:T(1,128)S(1)} %get-tuple-element.278), kind=kOutput, calls=%fused_computation.6 | convolution fusion | flops 57507840 | bytes 6684816 | tf_op jit(solution)/shard_map/vu,vxyz->uxyz/dot_general | solution.py:50
  174.1 15.7 %bitcast_add_fusion.7 = f32[6,8,128,128]{3,0,2,1:T(8,128)} fusion(f32[1,6,8,128,128]{4,3,2,1,0:T(8,128)S(1)} %copy-done.4, f32[8,128,128,6]{2,3,1,0:T(8,128)} %fusion.23, f32[8,128,128,6]{2,3,1,0:T(8,128)} %fusion.25, f32[8,128,128,6]{2,3,1,0:T(8,128)} %fusion.31, f32[8,128,128,6]{2,3,1,0:T(8,128)} %fusion.33, f32[6,8,128,128]{3,0,2,1:T(8,128)} %fusion.70, ...), kind=kOutput, calls=%fused_computation.33 | convolution fusion | flops 63799296 | bytes 29229200 | tf_op jit(solution)/shard_map/vu,vxyz->uxyz/dot_general | solution.py:50
  189.9 3.2 fusion.66
  193.2 6.7 %scatter_fusion = f32[6,1024,128]{2,0,1:T(8,128)} fusion(f32[6,1024,128]{2,0,1:T(8,128)} %bitcast.1218, s32[64]{0:T(128)S(1)} %fusion.82, f32[64,6,128]{2,1,0:T(8,128)S(1)} %copy.724), kind=kCustom, calls=%fused_computation.4 | custom fusion | flops 49152 | bytes 590080 | tf_op jit(solution)/shard_map/scatter-add | solution.py:68
  206.1 5.2 %fusion.27 = f32[8,128,128,6]{2,3,1,0:T(8,128)} fusion(f32[6,8,128,128]{3,0,2,1:T(8,128)S(1)} %fusion.69, f32[1,1,6,6]{3,0,2,1:T(1,128)S(1)} %get-tuple-element.276), kind=kOutput, calls=%fused_computation.49 | convolution fusion | flops 56180736 | bytes 7310336 | tf_op jit(solution)/shard_map/vu,vxyz->uxyz/dot_general | solution.py:50
  211.3 5.2 %fusion.29 = f32[8,128,128,6]{2,3,1,0:T(8,128)} fusion(f32[6,8,128,128]{3,0,2,1:T(8,128)S(1)} %fusion.69, f32[1,1,6,6]{3,0,2,1:T(1,128)S(1)} %get-tuple-element.277), kind=kOutput, calls=%fused_computation.51 | convolution fusion | flops 56180736 | bytes 7310336 | tf_op jit(solution)/shard_map/vu,vxyz->uxyz/dot_general | solution.py:50
  216.5 5.8 %fusion.76 = f32[6,8,128,128]{3,0,2,1:T(8,128)} fusion(f32[6,8,128,128]{3,0,2,1:T(8,128)S(1)} %fusion.69, f32[6,6]{1,0:T(8,128)S(1)} %reduce_sum.8), kind=kOutput, calls=%fused_computation.602 | convolution fusion | flops 56623140 | bytes 6291600 | tf_op jit(solution)/shard_map/vu,vxyz->uxyz/dot_general | solution.py:50
  224.9 5.4 %fusion.21 = f32[8,128,128,6]{2,3,1,0:T(8,128)} fusion(f32[6,8,128,127]{3,0,2,1:T(8,128)S(1)} %get-tuple-element.138, f32[1,1,6,6]{3,0,2,1:T(1,128)S(1)} %get-tuple-element.275), kind=kOutput, calls=%fused_computation.43 | convolution fusion | flops 56623104 | bytes 6267024 | tf_op jit(solution)/shard_map/vu,vxyz->uxyz/dot_general | solution.py:50
  230.3 2.9 collective-permute-start.3
  233.2 5.9 %fusion.19 = f32[8,128,128,6]{2,3,1,0:T(8,128)} fusion(f32[6,8,128,127]{3,0,2,1:T(8,128)S(1)} %get-tuple-element.139, f32[1,1,6,6]{3,0,2,1:T(1,128)S(1)} %get-tuple-element.279), kind=kOutput, calls=%fused_computation.41 | convolution fusion | flops 56623104 | bytes 6267024 | tf_op jit(solution)/shard_map/vu,vxyz->uxyz/dot_general | solution.py:50
  239.2 5.9 %fusion.8 = f32[8,128,128,6]{2,3,1,0:T(8,128)} fusion(f32[6,1,128,128]{3,0,2,1:T(8,128)S(1)} %collective-permute-done.2, f32[6,8,128,128]{3,0,2,1:T(8,128)S(1)} %fusion.69, f32[1,1,6,6]{3,0,2,1:T(1,128)S(1)} %get-tuple-element.278), kind=kOutput, calls=%fused_computation.14 | convolution fusion | flops 57507840 | bytes 6684816 | tf_op jit(solution)/shard_map/vu,vxyz->uxyz/dot_general | solution.py:50
  245.0 14.1 %fusion.17 = f32[6,8,128,128]{3,0,2,1:T(8,128)} fusion(f32[8,128,128,6]{2,3,1,0:T(8,128)} %fusion.19, f32[8,128,128,6]{2,3,1,0:T(8,128)} %fusion.21, f32[8,128,128,6]{2,3,1,0:T(8,128)} %fusion.27, f32[8,128,128,6]{2,3,1,0:T(8,128)} %fusion.29, f32[6,8,128,128]{3,0,2,1:T(8,128)} %fusion.76, f32[8,128,128,6]{2,3,1,0:T(8,128)} %fusion.8, ...), kind=kOutput, calls=%fused_computation.26 | convolution fusion | flops 63799296 | bytes 29229200 | tf_op jit(solution)/shard_map/vu,vxyz->uxyz/dot_general | solution.py:50
  259.1 8.0 %bitcast_add_fusion.14 = (f32[6,1024,128]{2,0,1:T(8,128)}, f32[6,1024,128]{2,0,1:T(8,128)}) fusion(f32[1,6,8,128,128]{4,1,3,2,0:T(8,128)S(1)} %copy-done.2, f32[6,1024,128]{2,0,1:T(8,128)} %scatter_fusion, f32[6,8,128,128]{3,0,2,1:T(8,128)} %fusion.17), kind=kLoop, calls=%fused_computation.616 | loop fusion | flops 2359296 | bytes 15728640 | tf_op jit(solution)/shard_map/add | solution.py:96
  267.1 10.4 %gather_fusion.3 = f32[1024,6,128]{2,1,0:T(8,128)} fusion(f32[6,1024,128]{2,0,1:T(8,128)} %get-tuple-element.134, s32[1024]{0:T(1024)S(1)} %fusion.81), kind=kCustom, calls=%fused_computation.1.clone | custom fusion | bytes 6295552 | tf_op jit(solution)/shard_map/jit(_take)/gather | solution.py:31
  277.5 7.6 %bitcast_multiply_fusion = f32[6,1024,128]{2,0,1:T(8,128)S(1)} fusion(f32[1024,6,128]{2,1,0:T(8,128)} %gather_fusion.3, f32[1024]{0:T(1024)S(1)} %broadcast_select_fusion, pred[1024]{0:T(1024)(128)(4,1)S(1)} %compare_and_fusion), kind=kLoop, calls=%fused_computation.22 | loop fusion | flops 1572864 | bytes 6296576 | tf_op jit(solution)/shard_map/mul | solution.py:34
  364.1 14.1 %all-to-all-start.1 = ((f32[128,6,1,8,128]{4,3,1,2,0:T(8,128)}), f32[128,6,1,8,128]{4,3,1,2,0:T(8,128)}, u32[]{:S(2)}, u32[]{:S(2)}) async-start(f32[128,6,1,8,128]{4,3,1,2,0:T(8,128)} %constant_dynamic-update-slice_fusion.128), calls=%async_computation.1 | async-start | bytes 6291456 | tf_op jit(solution)/shard_map/all_to_all | solution.py:38
  378.2 2.8 gather_fusion.1
  381.0 38.8 %all-to-all-done.1 = f32[128,6,1,8,128]{4,3,1,2,0:T(8,128)} async-done(((f32[128,6,1,8,128]{4,3,1,2,0:T(8,128)}), f32[128,6,1,8,128]{4,3,1,2,0:T(8,128)}, u32[]{:S(2)}, u32[]{:S(2)}) %all-to-all-start.1) | async-done | bytes 3145760 | tf_op jit(solution)/shard_map/all_to_all | solution.py:38
  419.7 3.2 fusion.57
  423.0 6.8 %scatter_fusion.1 = f32[6,1024,128]{2,0,1:T(8,128)} fusion(f32[6,1024,128]{2,0,1:T(8,128)} %get-tuple-element.135, s32[64]{0:T(128)S(1)} %fusion.82, f32[64,6,128]{2,1,0:T(8,128)S(1)} %copy.862), kind=kCustom, calls=%fused_computation.5 | custom fusion | flops 49152 | bytes 590080 | tf_op jit(solution)/shard_map/scatter-add | solution.py:68
  (327 shorter events, 178.5 us)
Async XLA Ops:
  0.9 5.7 %copy-start.9 = (f32[1,128,8]{1,2,0:T(8,128)S(1)}, f32[1,128,8]{1,2,0:T(8,128)}, u32[]{:S(2)}) copy-start(f32[1,128,8]{1,2,0:T(8,128)} %param.17) | copy-start | bytes 12292
  0.9 5.9 %copy-start.11 = (s32[1,128]{1,0:T(1,128)S(1)}, s32[1,128]{1,0:T(1,128)}, u32[]{:S(2)}) copy-start(s32[1,128]{1,0:T(1,128)} %param.16) | copy-start | bytes 1540
  103.6 86.2 %all-to-all-start = ((f32[128,6,1,8,128]{4,3,1,2,0:T(8,128)}), f32[128,6,1,8,128]{4,3,1,2,0:T(8,128)}, u32[]{:S(2)}, u32[]{:S(2)}) async-start(f32[128,6,1,8,128]{4,3,1,2,0:T(8,128)} %constant_dynamic-update-slice_fusion), calls=%async_computation | async-start | bytes 6291456 | tf_op jit(solution)/shard_map/all_to_all | solution.py:38
  117.8 48.1 %collective-permute-start = (f32[6,1,128,128]{3,0,2,1:T(8,128)}, f32[6,1,128,128]{3,0,2,1:T(8,128)}, u32[]{:S(2)}, u32[]{:S(2)}) collective-permute-start(f32[6,1,128,128]{3,0,2,1:T(8,128)} %get-tuple-element.269), channel_id=1, source_target_pairs={{1,0},{2,1},{3,2},{4,3},{5,4},{6,5},{7,6},{8,7},{9,8},{10,9},{11,1... | collective-permute-start | bytes 1179656 | tf_op jit(solution)/shard_map/ppermute | solution.py:20
  120.9 9.7 %copy-start.8 = (f32[1,6,6,6]{3,0,2,1:T(1,128)S(1)}, f32[1,6,6,6]{3,0,2,1:T(1,128)}, u32[]{:S(2)}) copy-start(f32[1,6,6,6]{3,0,2,1:T(1,128)} %param.14) | copy-start | bytes 2596
  120.9 9.7 %copy-start = (f32[1,6,8,128,128]{4,1,3,2,0:T(8,128)S(1)}, f32[1,6,8,128,128]{4,1,3,2,0:T(8,128)}, u32[]{:S(2)}) copy-start(f32[1,6,8,128,128]{4,1,3,2,0:T(8,128)} %copy.1974) | copy-start | bytes 9437188
  120.9 53.2 %collective-permute-start.1 = (f32[6,1,128,128]{3,0,2,1:T(8,128)}, f32[6,1,128,128]{3,0,2,1:T(8,128)}, u32[]{:S(2)}, u32[]{:S(2)}) collective-permute-start(f32[6,1,128,128]{3,0,2,1:T(8,128)} %get-tuple-element.268), channel_id=1, source_target_pairs={{0,1},{1,2},{2,3},{3,4},{4,5},{5,6},{6,7},{7,8},{8,9},{9,10},{10,1... | collective-permute-start | bytes 1179656 | tf_op jit(solution)/shard_map/ppermute | solution.py:18
  136.0 5.8 %copy-start.12 = (s32[1,64]{1,0:T(1,128)S(1)}, s32[1,64]{1,0:T(1,128)}, u32[]{:S(2)}) copy-start(s32[1,64]{1,0:T(1,128)} %param.19) | copy-start | bytes 772
  141.8 8.0 %copy-start.3 = (f32[1,6,8,128,128]{4,3,2,1,0:T(8,128)S(1)}, f32[1,6,8,128,128]{4,3,2,1,0:T(8,128)}, u32[]{:S(2)}) copy-start(f32[1,6,8,128,128]{4,3,2,1,0:T(8,128)} %param.11) | copy-start | bytes 9437188
  149.8 7.2 %copy-start.5 = (f32[6,8,128,127]{3,0,2,1:T(8,128)S(1)}, f32[6,8,128,127]{3,0,2,1:T(8,128)}, u32[]{:S(2)}) copy-start(f32[6,8,128,127]{3,0,2,1:T(8,128)} %get-tuple-element.270) | copy-start | bytes 9363460
  157.1 8.6 %copy-start.10 = (s32[1,128,8]{1,2,0:T(8,128)S(1)}, s32[1,128,8]{1,2,0:T(8,128)}, u32[]{:S(2)}) copy-start(s32[1,128,8]{1,2,0:T(8,128)} %param.18) | copy-start | bytes 12292
  165.9 8.2 %copy-start.1 = (f32[1,6,8,128,128]{4,1,3,2,0:T(8,128)S(1)}, f32[1,6,8,128,128]{4,1,3,2,0:T(8,128)}, u32[]{:S(2)}) copy-start(f32[1,6,8,128,128]{4,1,3,2,0:T(8,128)} %copy.1974) | copy-start | bytes 9437188
  165.9 8.2 %copy-start.4 = (f32[1,6,8,128,128]{4,3,2,1,0:T(8,128)S(1)}, f32[1,6,8,128,128]{4,3,2,1,0:T(8,128)}, u32[]{:S(2)}) copy-start(f32[1,6,8,128,128]{4,3,2,1,0:T(8,128)} %param.12) | copy-start | bytes 9437188
  165.9 8.2 %copy-start.6 = (f32[1,8,128,128]{3,2,1,0:T(8,128)S(1)}, f32[1,8,128,128]{3,2,1,0:T(8,128)}, u32[]{:S(2)}) copy-start(f32[1,8,128,128]{3,2,1,0:T(8,128)} %param.13) | copy-start | bytes 1572868
  222.3 16.9 %collective-permute-start.2 = (f32[6,1,128,128]{3,0,2,1:T(8,128)S(1)}, f32[6,1,128,128]{3,0,2,1:T(8,128)S(1)}, u32[]{:S(2)}, u32[]{:S(2)}) collective-permute-start(f32[6,1,128,128]{3,0,2,1:T(8,128)S(1)} %get-tuple-element.137), channel_id=1, source_target_pairs={{1,0},{2,1},{3,2},{4,3},{5,4},{6,5},{7,6},{8,7},{9,8},{10,9},{11,1... | collective-permute-start | bytes 1179656 | tf_op jit(solution)/shard_map/ppermute | solution.py:20
  230.3 14.7 %collective-permute-start.3 = (f32[6,1,128,128]{3,0,2,1:T(8,128)S(1)}, f32[6,1,128,128]{3,0,2,1:T(8,128)S(1)}, u32[]{:S(2)}, u32[]{:S(2)}) collective-permute-start(f32[6,1,128,128]{3,0,2,1:T(8,128)S(1)} %get-tuple-element.136), channel_id=1, source_target_pairs={{0,1},{1,2},{2,3},{3,4},{4,5},{5,6},{6,7},{7,8},{8,9},{9,10},{10,1... | collective-permute-start | bytes 1179656 | tf_op jit(solution)/shard_map/ppermute | solution.py:18
  239.2 5.9 %copy-start.7 = (f32[1,8,128,128]{3,2,1,0:T(8,128)S(1)}, f32[1,8,128,128]{3,2,1,0:T(8,128)}, u32[]{:S(2)}) copy-start(f32[1,8,128,128]{3,2,1,0:T(8,128)} %param.13) | copy-start | bytes 1572868
  245.0 14.1 %copy-start.2 = (f32[1,6,8,128,128]{4,1,3,2,0:T(8,128)S(1)}, f32[1,6,8,128,128]{4,1,3,2,0:T(8,128)}, u32[]{:S(2)}) copy-start(f32[1,6,8,128,128]{4,1,3,2,0:T(8,128)} %copy.1974) | copy-start | bytes 9437188
  364.1 55.6 %all-to-all-start.1 = ((f32[128,6,1,8,128]{4,3,1,2,0:T(8,128)}), f32[128,6,1,8,128]{4,3,1,2,0:T(8,128)}, u32[]{:S(2)}, u32[]{:S(2)}) async-start(f32[128,6,1,8,128]{4,3,1,2,0:T(8,128)} %constant_dynamic-update-slice_fusion.128), calls=%async_computation.1 | async-start | bytes 6291456 | tf_op jit(solution)/shard_map/all_to_all | solution.py:38
